TPU v7x, 256 devices: a whole 4x4x8 slice. The times are simulated.
256 devices in a mesh: dp: 32 (over z, x_hi, core), seq: 8 (over y, x_lo).
Axes of the slice: x: 4 (x_hi: 2, x_lo: 2; x = x_hi * 2 + x_lo), y: 4, z: 8, core: 2. Of those that a mesh axis runs over, the one named last changes fastest.
Arguments:
- grad_out: bfloat16 [32, 1024, 6144], P('dp', 'seq'), may hold values from -6 to 6
- queries: bfloat16 [32, 1024, 3072], P('dp', 'seq'), may hold values from -40 to 40
- keys: bfloat16 [32, 1024, 3072], P('dp', 'seq'), may hold values from -12 to 12
- values: bfloat16 [32, 1024, 3072], P('dp', 'seq'), may hold values from -6 to 6
- out_weight: bfloat16 [6144, 3072], P('dp', 'seq'), may hold values from -0.109375 to 0.109375
Outputs:
- query_grad: bfloat16 [32, 1024, 3072], P('dp', 'seq')
- key_grad: bfloat16 [32, 1024, 3072], P('dp', 'seq')
- value_grad: bfloat16 [32, 1024, 3072], P('dp', 'seq')
- weight_grad: float32 [6144, 3072], P('dp', 'seq')
All inputs are finite; a program needn't handle non-finite values.
Results may differ from a plain program's by a relative error of at most 0.03.
Values may be sent and summed in bfloat16 or wider, within the bound.
A program may use at most 128 MiB of HBM per device.

v0:
```python
import math
import jax
import jax.numpy as jnp
from jax import lax
from jax.sharding import PartitionSpec as P

HEAD_DIM = 128


def shards(grad_out, queries, keys, values, out_weight):
    gathered = lax.all_gather(grad_out, "seq", axis=1, tiled=True)[0]
    length = gathered.shape[0]
    features = out_weight.shape[1]
    heads_here = features // HEAD_DIM
    whole_rows = lax.all_gather(out_weight, "dp", axis=0, tiled=True)
    d_full = jnp.dot(gathered, whole_rows, preferred_element_type=jnp.float32)
    d_attn = d_full.astype(jnp.bfloat16)
    query_all, key_all, value_all = (
        lax.all_to_all(queries, "seq", split_axis=2, concat_axis=1, tiled=True),
        lax.all_to_all(keys, "seq", split_axis=2, concat_axis=1, tiled=True),
        lax.all_to_all(values, "seq", split_axis=2, concat_axis=1, tiled=True),
    )
    head_shape = (length, heads_here, HEAD_DIM)
    query_heads = query_all[0].reshape(head_shape)
    key_heads = key_all[0].reshape(head_shape)
    value_heads = value_all[0].reshape(head_shape)
    grad_heads = d_attn.reshape(head_shape)
    block_rows = math.gcd(length, 512)
    block_count = length // block_rows
    block_shape = (block_count, block_rows, heads_here, HEAD_DIM)
    query_blocks = query_heads.reshape(block_shape)
    grad_blocks = grad_heads.reshape(block_shape)
    inverse_root = 1.0 / math.sqrt(HEAD_DIM)
    token_scale = 1.0 / math.sqrt(lax.axis_size("dp") * length)

    def softmax_rows(query_block):
        scores = (
            jnp.einsum("qhd,khd->hqk", query_block, key_heads, preferred_element_type=jnp.float32)
            * inverse_root
        )
        largest = jnp.max(scores, axis=-1, keepdims=True)
        raised = jnp.exp(scores - largest)
        probabilities = raised / jnp.sum(raised, axis=-1, keepdims=True)
        return (probabilities, probabilities.astype(jnp.bfloat16))

    def attend(probs_low):
        return jnp.einsum(
            "hqk,khd->qhd", probs_low, value_heads, preferred_element_type=jnp.float32
        ).astype(jnp.bfloat16)

    def backward(totals, probabilities, probs_low, attended, query_block, grad_block):
        key_sums, value_sums = totals
        value_sums = value_sums + jnp.einsum(
            "hqk,qhd->khd", probs_low, grad_block, preferred_element_type=jnp.float32
        )
        d_probs = jnp.einsum(
            "qhd,khd->hqk", grad_block, value_heads, preferred_element_type=jnp.float32
        )
        row_delta = jnp.sum(grad_block.astype(jnp.float32) * attended.astype(jnp.float32), axis=-1)
        d_scores = probabilities * (d_probs - jnp.transpose(row_delta)[:, :, None])
        scores_low = d_scores.astype(jnp.bfloat16)
        query_part = (
            jnp.einsum("hqk,khd->qhd", scores_low, key_heads, preferred_element_type=jnp.float32)
            * inverse_root
        ).astype(jnp.bfloat16)
        key_sums = key_sums + jnp.einsum(
            "hqk,qhd->khd", scores_low, query_block, preferred_element_type=jnp.float32
        )
        return ((key_sums, value_sums), query_part)

    zero_sums = (jnp.zeros(head_shape, jnp.float32), jnp.zeros(head_shape, jnp.float32))

    def advance(totals, pieces):
        query_block, grad_block = pieces
        probabilities, probs_low = softmax_rows(query_block)
        attended = attend(probs_low)
        totals, query_part = backward(
            totals, probabilities, probs_low, attended, query_block, grad_block
        )
        return (totals, (query_part, attended))

    (key_sums, value_sums), (query_parts, attended_blocks) = lax.scan(
        advance, zero_sums, (query_blocks, grad_blocks)
    )
    attended_all = attended_blocks.reshape(length, features)
    product = lax.dot_general(
        gathered, attended_all, (((0,), (0,)), ((), ())), preferred_element_type=jnp.float32
    )
    weight_grad = lax.psum_scatter(
        (product * token_scale).astype(jnp.bfloat16), "dp", scatter_dimension=0, tiled=True
    ).astype(jnp.float32)
    query_local = query_parts.reshape(1, length, features)
    key_local = (key_sums * inverse_root).astype(jnp.bfloat16).reshape(1, length, features)
    value_local = value_sums.astype(jnp.bfloat16).reshape(1, length, features)
    query_grad, key_grad, value_grad = (
        lax.all_to_all(query_local, "seq", split_axis=1, concat_axis=2, tiled=True),
        lax.all_to_all(key_local, "seq", split_axis=1, concat_axis=2, tiled=True),
        lax.all_to_all(value_local, "seq", split_axis=1, concat_axis=2, tiled=True),
    )
    return (query_grad, key_grad, value_grad, weight_grad)


def solution(mesh):
    in_specs = (
        P("dp", "seq", None),
        P("dp", "seq", None),
        P("dp", "seq", None),
        P("dp", "seq", None),
        P("dp", "seq"),
    )
    out_specs = (P("dp", "seq", None), P("dp", "seq", None), P("dp", "seq", None), P("dp", "seq"))
    return jax.shard_map(shards, mesh=mesh, in_specs=in_specs, out_specs=out_specs, check_vma=False)
```

profile of v0, /device:TPU:8, one launch (start us, length us, event | category | flops | bytes accessed | tf_op | source)
XLA Modules:
  0.0 578.9 jit_solution(2107303295354958740)
XLA Ops:
  8.6 3.7 copy.111
  12.8 16.9 %reduce = bf16[3072,128]{1,0:T(8,128)(2,1)S(1)} reduce(bf16[3072,1,128]{2,1,0:T(2,128)(2,1)S(1)} %bitcast.154, bf16[]{:T(256)} %broadcast.43), dimensions={1}, to_apply=%bitcast.87.reduce_sub_computation | reduce | bytes 1572866
  30.7 5.8 %all-to-all-start = ((bf16[8,2,24576]{2,1,0:T(2,128)(2,1)}), bf16[8,2,24576]{2,1,0:T(2,128)(2,1)S(1)}, u32[]{:S(2)}, u32[]{:S(2)}) async-start(bf16[8,2,24576]{2,1,0:T(2,128)(2,1)} %reshape.34), calls=%async_computation | async-start | bytes 1572864 | tf_op jit(solution)/shard_map/all_to_all | solution.py:19
  36.6 3.7 copy.113
  40.3 16.9 %reduce.1 = bf16[3072,128]{1,0:T(8,128)(2,1)S(1)} reduce(bf16[3072,1,128]{2,1,0:T(2,128)(2,1)S(1)} %bitcast.164, bf16[]{:T(256)} %broadcast.43), dimensions={1}, to_apply=%bitcast.89.reduce_sub_computation | reduce | bytes 1572866
  58.2 5.9 %all-to-all-start.1 = ((bf16[8,2,24576]{2,1,0:T(2,128)(2,1)}), bf16[8,2,24576]{2,1,0:T(2,128)(2,1)}, u32[]{:S(2)}, u32[]{:S(2)}) async-start(bf16[8,2,24576]{2,1,0:T(2,128)(2,1)} %reshape.36), calls=%async_computation.1 | async-start | bytes 1572864 | tf_op jit(solution)/shard_map/all_to_all | solution.py:20
  64.1 3.7 copy.116
  67.8 16.9 %reduce.2 = bf16[3072,128]{1,0:T(8,128)(2,1)S(1)} reduce(bf16[3072,1,128]{2,1,0:T(2,128)(2,1)S(1)} %bitcast.165, bf16[]{:T(256)} %broadcast.43), dimensions={1}, to_apply=%bitcast.91.reduce_sub_computation | reduce | bytes 1572866
  85.8 5.7 all-to-all-start.2
  91.5 5.5 reshape.35
  105.7 5.5 reshape.37
  118.6 5.5 reshape.39
  129.2 229.8 %all-gather.3.cloned.1.call-done = bf16[1,1024,6144]{2,1,0:T(8,128)(2,1)} async-done(((bf16[1,128,6144]{2,1,0:T(8,128)(2,1)}), bf16[1,1024,6144]{2,1,0:T(8,128)(2,1)}) %all-gather.3.cloned.1.call-update) | async-done | bytes 12582928 | tf_op jit(solution)/shard_map/all_gather | solution.py:11
  359.0 11.7 %fusion.45 = bf16[1024,384]{1,0:T(8,128)(2,1)} fusion(bf16[6144,384]{1,0:T(8,128)(2,1)} %all-gather.5.cloned.1.call-done, bf16[1,1024,6144]{2,1,0:T(8,128)(2,1)} %all-gather.3.cloned.1.call-done), kind=kOutput, calls=%fused_computation.42 | convolution fusion | flops 4832231424 | bytes 18087936 | tf_op jit(solution)/shard_map/dot_general | solution.py:16
  370.8 3.2 reshape.30
  376.2 35.0 %while.17 = (s32[]{:T(128)}, f32[1024,3,128]{0,2,1:T(8,128)S(1)}, f32[1024,3,128]{0,2,1:T(8,128)S(1)}, bf16[2,512,3,128]{3,1,2,0:T(8,128)(2,1)}, bf16[2,512,3,12...) while((s32[]{:T(128)}, f32[1024,3,128]{0,2,1:T(8,128)S(1)}, ...), condition=%wide.region_4.5_spmd.clone, body=%wide.region_0.4_spmd.clone.sunk | while | flops 2433023488 | bytes 94800312 | solution.py:82
  376.4 5.8 %fusion.91 = (f32[3,512]{1,0:T(4,128)S(1)}, f32[3,512,1024]{2,1,0:T(8,128)}) fusion(bf16[1024,3,128]{2,0,1:T(8,128)(2,1)} %get-tuple-element.279, bf16[2,512,3,128]{3,1,2,0:T(8,128)(2,1)} %get-tuple-element.278, s32[]{:T(128)S(6)} %copy.157), kind=kOutput, calls=%fused_computation.43.clone.1 | convolution fusion | flops 407372800 | bytes 7477252 | tf_op jit(solution)/shard_map/while/body/eval_jaxpr/sub | solution.py:42
  382.2 3.6 fusion.92
  393.9 5.8 %fusion.91 = (f32[3,512]{1,0:T(4,128)S(1)}, f32[3,512,1024]{2,1,0:T(8,128)}) fusion(bf16[1024,3,128]{2,0,1:T(8,128)(2,1)} %get-tuple-element.279, bf16[2,512,3,128]{3,1,2,0:T(8,128)(2,1)} %get-tuple-element.278, s32[]{:T(128)S(6)} %copy.157), kind=kOutput, calls=%fused_computation.43.clone.1 | convolution fusion | flops 407372800 | bytes 7477252 | tf_op jit(solution)/shard_map/while/body/eval_jaxpr/sub | solution.py:42
  399.7 3.6 fusion.92
  415.6 11.3 %fusion.42 = bf16[6144,384]{0,1:T(8,128)(2,1)} fusion(bf16[1024,384]{0,1:T(8,128)(2,1)S(1)} %bitcast.178, bf16[1,1024,6144]{2,1,0:T(8,128)(2,1)} %all-gather.3.cloned.1.call-done), kind=kOutput, calls=%fused_computation.40 | convolution fusion | flops 4836556800 | bytes 18087936 | tf_op jit(solution)/shard_map/dot_general | solution.py:86
  426.9 6.6 %copy.140 = bf16[6144,384]{1,0:T(8,128)(2,1)} copy(bf16[6144,384]{0,1:T(8,128)(2,1)} %fusion.42) | data formatting | bytes 9437184
  434.6 4.5 copy.124
  439.1 6.2 %reduce.4 = bf16[1024,384]{1,0:T(8,128)(2,1)} reduce(bf16[1024,1,384]{2,1,0:T(2,128)(2,1)S(1)} %bitcast.159, bf16[]{:T(256)} %broadcast.43), dimensions={1}, to_apply=%bitcast.95.reduce_sub_computation | reduce | bytes 1572866
  448.2 5.5 all-to-all-start.4
  456.0 5.3 reduce.5
  464.5 6.2 %all-to-all-start.5 = ((bf16[8,2,24576]{2,1,0:T(2,128)(2,1)}), bf16[8,2,24576]{2,1,0:T(2,128)(2,1)}, u32[]{:S(2)}, u32[]{:S(2)}) async-start(bf16[8,2,24576]{2,1,0:T(2,128)(2,1)} %reshape.44), calls=%async_computation.5 | async-start | bytes 1572864 | tf_op jit(solution)/shard_map/all_to_all | solution.py:98
  472.2 5.3 reduce.3
  480.4 5.6 all-to-all-start.3
  488.5 4.1 reshape.45
  494.3 8.4 %all-to-all-done.3 = bf16[8,2,24576]{2,1,0:T(2,128)(2,1)S(1)} async-done(((bf16[8,2,24576]{2,1,0:T(2,128)(2,1)}), bf16[8,2,24576]{2,1,0:T(2,128)(2,1)S(1)}, u32[]{:S(2)}, u32[]{:S(2)}) %all-to-all-start.3) | async-done | bytes 786464 | tf_op jit(solution)/shard_map/all_to_all | solution.py:96
  505.2 65.1 %reduce-scatter.4.cloned.1.call-done = bf16[192,384]{1,0:T(8,128)(2,1)} async-done(((bf16[6144,384]{1,0:T(8,128)(2,1)}), bf16[192,384]{1,0:T(8,128)(2,1)}) %reduce-scatter.4.cloned.1.call-update) | async-done | bytes 147472
  (113 shorter events, 70.8 us)
Async XLA Ops:
  7.2 122.1 %all-gather.5.cloned.1.call-start = ((), (), s32[]{:S(2)}) async-start(), calls=%async_computation.8 | async-start | bytes 4866048 | tf_op jit(solution)/shard_map/all_gather | solution.py:15
  7.9 351.1 %all-gather.3.cloned.1.call-start = ((), (), s32[]{:S(2)}) async-start(), calls=%async_computation.7 | async-start | bytes 14155776 | tf_op jit(solution)/shard_map/all_gather | solution.py:11
  30.7 27.5 %all-to-all-start = ((bf16[8,2,24576]{2,1,0:T(2,128)(2,1)}), bf16[8,2,24576]{2,1,0:T(2,128)(2,1)S(1)}, u32[]{:S(2)}, u32[]{:S(2)}) async-start(bf16[8,2,24576]{2,1,0:T(2,128)(2,1)} %reshape.34), calls=%async_computation | async-start | bytes 1572864 | tf_op jit(solution)/shard_map/all_to_all | solution.py:19
  58.2 26.5 %copy-start.2 = (bf16[8,2,24576]{2,1,0:T(2,128)(2,1)}, bf16[8,2,24576]{2,1,0:T(2,128)(2,1)S(1)}, u32[]{:S(2)}) copy-start(bf16[8,2,24576]{2,1,0:T(2,128)(2,1)S(1)} %all-to-all-done) | copy-start | bytes 2359300
  58.2 27.6 %all-to-all-start.1 = ((bf16[8,2,24576]{2,1,0:T(2,128)(2,1)}), bf16[8,2,24576]{2,1,0:T(2,128)(2,1)}, u32[]{:S(2)}, u32[]{:S(2)}) async-start(bf16[8,2,24576]{2,1,0:T(2,128)(2,1)} %reshape.36), calls=%async_computation.1 | async-start | bytes 1572864 | tf_op jit(solution)/shard_map/all_to_all | solution.py:20
  85.8 32.9 %all-to-all-start.2 = ((bf16[8,2,24576]{2,1,0:T(2,128)(2,1)}), bf16[8,2,24576]{2,1,0:T(2,128)(2,1)}, u32[]{:S(2)}, u32[]{:S(2)}) async-start(bf16[8,2,24576]{2,1,0:T(2,128)(2,1)} %reshape.38), calls=%async_computation.2 | async-start | bytes 1572864 | tf_op jit(solution)/shard_map/all_to_all | solution.py:21
  91.5 478.8 %reduce-scatter.4.cloned.1.call-start = ((), (), s32[]{:S(2)}) async-start(), calls=%async_computation.9 | async-start | bytes 4866048
  382.2 3.6 copy-start.1
  382.2 3.6 copy-start.7
  385.9 2.2 slice-start
  387.0 2.0 slice-start.1
  389.0 1.2 copy-start.3
  389.0 1.4 copy-start.6
  390.4 1.1 copy-start
  391.5 1.0 copy-start.4
  391.5 1.4 copy-start.8
  393.0 0.9 copy-start.9
  399.7 3.6 copy-start.1
  399.7 3.6 copy-start.7
  403.3 2.2 slice-start
  404.4 2.0 slice-start.1
  406.4 1.2 copy-start.3
  406.4 1.4 copy-start.6
  407.8 1.1 copy-start
  408.9 1.0 copy-start.4
  408.9 1.4 copy-start.8
  410.4 0.9 copy-start.9
  448.2 16.3 %all-to-all-start.4 = ((bf16[8,2,24576]{2,1,0:T(2,128)(2,1)}), bf16[8,2,24576]{2,1,0:T(2,128)(2,1)S(1)}, u32[]{:S(2)}, u32[]{:S(2)}) async-start(bf16[8,2,24576]{2,1,0:T(2,128)(2,1)} %reshape.42), calls=%async_computation.4 | async-start | bytes 1572864 | tf_op jit(solution)/shard_map/all_to_all | solution.py:97
  461.3 9.4 %copy-start.5 = (bf16[2,512,3,128]{3,1,2,0:T(8,128)(2,1)S(1)}, bf16[2,512,3,128]{3,1,2,0:T(8,128)(2,1)}, u32[]{:S(2)}) copy-start(bf16[2,512,3,128]{3,1,2,0:T(8,128)(2,1)} %get-tuple-element.54) | copy-start | bytes 2359300
  464.5 15.9 %all-to-all-start.5 = ((bf16[8,2,24576]{2,1,0:T(2,128)(2,1)}), bf16[8,2,24576]{2,1,0:T(2,128)(2,1)}, u32[]{:S(2)}, u32[]{:S(2)}) async-start(bf16[8,2,24576]{2,1,0:T(2,128)(2,1)} %reshape.44), calls=%async_computation.5 | async-start | bytes 1572864 | tf_op jit(solution)/shard_map/all_to_all | solution.py:98
  480.4 22.3 %all-to-all-start.3 = ((bf16[8,2,24576]{2,1,0:T(2,128)(2,1)}), bf16[8,2,24576]{2,1,0:T(2,128)(2,1)S(1)}, u32[]{:S(2)}, u32[]{:S(2)}) async-start(bf16[8,2,24576]{2,1,0:T(2,128)(2,1)} %reshape.40), calls=%async_computation.3 | async-start | bytes 1572864 | tf_op jit(solution)/shard_map/all_to_all | solution.py:96
Sparse Core Ops, SparseCore 0:
  10.8 100.1 all-gather.4
  112.8 246.2 all-gather.2
  433.7 136.5 reduce-scatter.3
where the time goes:
time: 589 us; the launch traced here: 579 us
  waiting for transfers between devices  309 us (52%)
  local copies, waits for them, and re-layouts  99.8 us (17%)
  other arithmetic  75.8 us (13%)
  matrix products  45.4 us (8%)
  starting transfers between devices  34.8 us (6%)
  between operations  14.2 us (2%)
    all_gather x1, waiting for transfers between devices, shards(): gathered = lax.all_gather(grad_out, 'seq', axis=1, tiled=True)[0]  230 us
    unnamed x36, local copies, waits for them, and re-layouts  67.8 us
    unnamed x8, other arithmetic  67.5 us
    unnamed x4, waiting for transfers between devices  66.5 us
  transfers between devices with their start and end apart: 9, of which 5 were waited for; matrix products, arithmetic and copies ran while one was open for 25% of the time, Pallas kernels for 0%

commit v1 on v0

--- a/solution.py
+++ b/solution.py
@@ -8,7 +8,9 @@
 
 
 def shards(grad_out, queries, keys, values, out_weight):
-    gathered = lax.all_gather(grad_out, "seq", axis=1, tiled=True)[0]
+    gathered = jnp.concatenate(
+        lax.all_to_all(jnp.stack([grad_out] * lax.axis_size("seq")), "seq", 0, 0), axis=1
+    )[0]
     length = gathered.shape[0]
     features = out_weight.shape[1]
     heads_here = features // HEAD_DIM

time: 589 us -> 497 us (0.84)
  waiting for transfers between devices: 309 us -> 208 us
  local copies, waits for them, and re-layouts: 99.8 us -> 79.2 us
  blocking collectives: 0 us -> 15.5 us
  matrix products: 45.4 us -> 56 us
    all_gather x1 -> x0, waiting for transfers between devices: 230 us -> none  [shards(): gathered = lax.all_gather(grad_out, 'seq', axis=1, tiled=True)[0]]
    all_gather x1, waiting for transfers between devices: 0.01 us -> 94.5 us  [shards(): whole_rows = lax.all_gather(out_weight, 'dp', axis=0, tiled=True)]
    all_to_all x1, waiting for transfers between devices: 0.01 us -> 41.6 us  [shards(): lax.all_to_all(jnp.stack([grad_out] * lax.axis_size('seq')), 'seq', 0, 0)]
    unnamed x36 -> x38, local copies, waits for them, and re-layouts: 67.8 us -> 50.9 us
    all_to_all x0 -> x1, blocking collectives: none -> 15.5 us  [shards(): lax.all_to_all(values, 'seq', split_axis=2, concat_axis=1, tiled=True)]
    all_to_all x1, waiting for transfers between devices: 8.36 us -> 0.01 us  [shards(): lax.all_to_all(query_local, 'seq', split_axis=1, concat_axis=2, tiled=True)]
    another operation x0 -> x1, local copies, waits for them, and re-layouts: none -> 7.45 us  [shards(): jnp.stack([grad_out] * lax.axis_size('seq'))]
    dot_general x2, matrix products: 1.92 us -> 8.4 us  [backward(): jnp.einsum('hqk,qhd->khd', scores_low, query_block, preferred_element_typ...]
  transfers between devices with their start and end apart: 9 -> 8, of which waited for: 5 -> 4; matrix products, arithmetic and copies ran while one was open for 25% -> 21% of each run, Pallas kernels for 0% -> 0%
where the time goes in v1:
time: 497 us; the launch traced here: 488 us
  waiting for transfers between devices  208 us (42%)
  local copies, waits for them, and re-layouts  79.2 us (16%)
  other arithmetic  77.6 us (16%)
  matrix products  56 us (11%)
  starting transfers between devices  37 us (7%)
  blocking collectives  15.5 us (3%)
  between operations  14.6 us (3%)
    all_gather x1, waiting for transfers between devices, shards(): whole_rows = lax.all_gather(out_weight, 'dp', axis=0, tiled=True)  94.5 us
    unnamed x8, other arithmetic  69.1 us
    unnamed x3, waiting for transfers between devices  66 us
    unnamed x38, local copies, waits for them, and re-layouts  50.9 us
    all_to_all x1, waiting for transfers between devices, shards(): lax.all_to_all(jnp.stack([grad_out] * lax.axis_size('seq')), 'seq', 0, 0)  41.6 us
    all_to_all x1, blocking collectives, shards(): lax.all_to_all(values, 'seq', split_axis=2, concat_axis=1, tiled=True)  15.5 us
    sub x2, matrix products, softmax_rows(): raised = jnp.exp(scores - largest)  11.6 us
    dot_general x1, matrix products, shards(): lax.dot_general(gathered, attended_all, (((0,), (0,)), ((), ())), preferr...  11.3 us
  transfers between devices with their start and end apart: 8, of which 4 were waited for; matrix products, arithmetic and copies ran while one was open for 21% of the time, Pallas kernels for 0%

profile of v1, /device:TPU:8, one launch (start us, length us, event | category | flops | bytes accessed | tf_op | source)
XLA Modules:
  0.0 487.8 jit_solution(5222936832079890006)
XLA Ops:
  11.4 16.9 %reduce = bf16[3072,128]{1,0:T(8,128)(2,1)S(1)} reduce(bf16[3072,1,128]{2,1,0:T(2,128)(2,1)S(1)} %bitcast.147, bf16[]{:T(256)} %broadcast.46), dimensions={1}, to_apply=%bitcast.78.reduce_sub_computation | reduce | bytes 1572866
  29.4 5.8 %all-to-all-start = ((bf16[8,2,24576]{2,1,0:T(2,128)(2,1)}), bf16[8,2,24576]{2,1,0:T(2,128)(2,1)S(1)}, u32[]{:S(2)}, u32[]{:S(2)}) async-start(bf16[8,2,24576]{2,1,0:T(2,128)(2,1)} %reshape.37), calls=%async_computation | async-start | bytes 1572864 | tf_op jit(solution)/shard_map/all_to_all | solution.py:21
  38.9 16.9 %reduce.1 = bf16[3072,128]{1,0:T(8,128)(2,1)S(1)} reduce(bf16[3072,1,128]{2,1,0:T(2,128)(2,1)S(1)} %bitcast.157, bf16[]{:T(256)} %broadcast.46), dimensions={1}, to_apply=%bitcast.80.reduce_sub_computation | reduce | bytes 1572866
  57.0 5.9 %all-to-all-start.1 = ((bf16[8,2,24576]{2,1,0:T(2,128)(2,1)}), bf16[8,2,24576]{2,1,0:T(2,128)(2,1)}, u32[]{:S(2)}, u32[]{:S(2)}) async-start(bf16[8,2,24576]{2,1,0:T(2,128)(2,1)} %reshape.39), calls=%async_computation.1 | async-start | bytes 1572864 | tf_op jit(solution)/shard_map/all_to_all | solution.py:22
  62.9 3.7 copy.116
  66.6 16.9 %reduce.2 = bf16[3072,128]{1,0:T(8,128)(2,1)S(1)} reduce(bf16[3072,1,128]{2,1,0:T(2,128)(2,1)S(1)} %bitcast.158, bf16[]{:T(256)} %broadcast.46), dimensions={1}, to_apply=%bitcast.82.reduce_sub_computation | reduce | bytes 1572866
  83.7 15.5 %all_to_all.104 = bf16[8,2,24576]{2,1,0:T(2,128)(2,1)S(1)} all-to-all(bf16[8,2,24576]{2,1,0:T(2,128)(2,1)S(1)} %reshape.41), channel_id=1, replica_groups=mesh['dp'=32,'seq'=8] {'seq'}, dimensions={0} | all-to-all | bytes 1572864 | tf_op jit(solution)/shard_map/all_to_all | solution.py:23
  99.2 7.5 %stack.2 = bf16[8,1,128,6144]{3,2,1,0:T(8,128)(2,1)} broadcast(bf16[128,6144]{1,0:T(8,128)(2,1)} %bitcast.171), dimensions={2,3} | broadcast | bytes 14155776 | tf_op jit(solution)/shard_map/stack | solution.py:12
  106.7 7.0 %all-to-all-start.2 = ((bf16[8,1,128,6144]{3,2,1,0:T(8,128)(2,1)}), bf16[8,1,128,6144]{3,2,1,0:T(8,128)(2,1)}, u32[]{:S(2)}, u32[]{:S(2)}) async-start(bf16[8,1,128,6144]{3,2,1,0:T(8,128)(2,1)} %stack.2), calls=%async_computation.2 | async-start | bytes 25165824 | tf_op jit(solution)/shard_map/all_to_all | solution.py:12
  118.1 4.1 reshape.40
  127.0 94.5 %all-gather.2.cloned.1.call-done = bf16[6144,384]{1,0:T(8,128)(2,1)} async-done(((bf16[192,384]{1,0:T(8,128)(2,1)}), bf16[6144,384]{1,0:T(8,128)(2,1)}) %all-gather.2.cloned.1.call-update) | async-done | bytes 4718608 | tf_op jit(solution)/shard_map/all_gather | solution.py:17
  221.6 41.6 %all-to-all-done.2 = bf16[8,1,128,6144]{3,2,1,0:T(8,128)(2,1)} async-done(((bf16[8,1,128,6144]{3,2,1,0:T(8,128)(2,1)}), bf16[8,1,128,6144]{3,2,1,0:T(8,128)(2,1)}, u32[]{:S(2)}, u32[]{:S(2)}) %all-to-all-start.2) | async-done | bytes 12582944 | tf_op jit(solution)/shard_map/all_to_all | solution.py:12
  263.2 11.0 %convolution_convert_fusion.1 = bf16[1024,384]{1,0:T(8,128)(2,1)S(1)} fusion(bf16[1024,6144]{1,0:T(8,128)(2,1)} %bitcast.3, bf16[6144,384]{1,0:T(8,128)(2,1)} %all-gather.2.cloned.1.call-done), kind=kOutput, calls=%fused_computation.38 | convolution fusion | flops 4832231424 | bytes 18087936 | tf_op jit(solution)/shard_map/dot_general | solution.py:18
  275.5 46.0 %while.17 = (s32[]{:T(128)}, f32[1024,3,128]{0,2,1:T(8,128)}, f32[1024,3,128]{0,2,1:T(8,128)}, bf16[2,512,3,128]{3,1,2,0:T(8,128)(2,1)}, bf16[2,512,3,128]{3,1,2...) while((s32[]{:T(128)}, f32[1024,3,128]{0,2,1:T(8,128)}, ...), condition=%wide.region_4.5_spmd.clone, body=%wide.region_0.4_spmd.clone.sunk | while | flops 2433023488 | bytes 110530456 | solution.py:84
  275.7 5.8 %fusion.82 = (f32[3,512]{1,0:T(4,128)S(1)}, f32[3,512,1024]{2,1,0:T(8,128)}) fusion(bf16[1024,3,128]{2,0,1:T(8,128)(2,1)} %get-tuple-element.279, bf16[2,512,3,128]{3,1,2,0:T(8,128)(2,1)} %get-tuple-element.278, s32[]{:T(128)} %get-tuple-element.262), kind=kOutput, calls=%fused_computation.39.clone.1 | convolution fusion | flops 407372800 | bytes 7477760 | tf_op jit(solution)/shard_map/while/body/eval_jaxpr/sub | solution.py:44
  281.5 3.7 fusion.83
  289.0 4.0 bitcast_add_fusion.4
  298.4 5.8 %fusion.82 = (f32[3,512]{1,0:T(4,128)S(1)}, f32[3,512,1024]{2,1,0:T(8,128)}) fusion(bf16[1024,3,128]{2,0,1:T(8,128)(2,1)} %get-tuple-element.279, bf16[2,512,3,128]{3,1,2,0:T(8,128)(2,1)} %get-tuple-element.278, s32[]{:T(128)} %get-tuple-element.262), kind=kOutput, calls=%fused_computation.39.clone.1 | convolution fusion | flops 407372800 | bytes 7477760 | tf_op jit(solution)/shard_map/while/body/eval_jaxpr/sub | solution.py:44
  304.2 3.7 fusion.83
  311.7 4.4 bitcast_add_fusion.4
  323.9 11.3 %fusion.36 = bf16[6144,384]{0,1:T(8,128)(2,1)} fusion(bf16[1024,384]{0,1:T(8,128)(2,1)S(1)} %bitcast.172, bf16[1024,6144]{1,0:T(8,128)(2,1)} %bitcast.3), kind=kOutput, calls=%fused_computation.36 | convolution fusion | flops 4836556800 | bytes 18087936 | tf_op jit(solution)/shard_map/dot_general | solution.py:88
  335.2 6.6 %copy.140 = bf16[6144,384]{1,0:T(8,128)(2,1)} copy(bf16[6144,384]{0,1:T(8,128)(2,1)} %fusion.36) | data formatting | bytes 9437184
  344.8 6.4 %reduce.3 = bf16[1024,384]{1,0:T(8,128)(2,1)} reduce(bf16[1024,1,384]{2,1,0:T(2,128)(2,1)S(1)} %bitcast.152, bf16[]{:T(256)} %broadcast.46), dimensions={1}, to_apply=%bitcast.84.reduce_sub_computation | reduce | bytes 1572866
  354.0 6.5 %all-to-all-start.4 = ((bf16[8,2,24576]{2,1,0:T(2,128)(2,1)}), bf16[8,2,24576]{2,1,0:T(2,128)(2,1)}, u32[]{:S(2)}, u32[]{:S(2)}) async-start(bf16[8,2,24576]{2,1,0:T(2,128)(2,1)} %reshape.43), calls=%async_computation.4 | async-start | bytes 1572864 | tf_op jit(solution)/shard_map/all_to_all | solution.py:98
  361.5 4.1 copy.124
  365.7 6.4 %reduce.4 = bf16[1024,384]{1,0:T(8,128)(2,1)} reduce(bf16[1024,1,384]{2,1,0:T(2,128)(2,1)S(1)} %bitcast.153, bf16[]{:T(256)} %broadcast.46), dimensions={1}, to_apply=%bitcast.86.reduce_sub_computation | reduce | bytes 1572866
  375.0 5.9 %all-to-all-start.5 = ((bf16[8,2,24576]{2,1,0:T(2,128)(2,1)}), bf16[8,2,24576]{2,1,0:T(2,128)(2,1)S(1)}, u32[]{:S(2)}, u32[]{:S(2)}) async-start(bf16[8,2,24576]{2,1,0:T(2,128)(2,1)} %reshape.45), calls=%async_computation.5 | async-start | bytes 1572864 | tf_op jit(solution)/shard_map/all_to_all | solution.py:99
  383.2 5.4 %reduce.5 = bf16[1024,384]{1,0:T(8,128)(2,1)S(1)} reduce(bf16[1024,1,384]{2,1,0:T(2,128)(2,1)S(1)} %bitcast.148, bf16[]{:T(256)} %broadcast.46), dimensions={1}, to_apply=%bitcast.88.reduce_sub_computation | reduce | bytes 1572866
  389.7 5.7 %all-to-all-start.6 = ((bf16[8,2,24576]{2,1,0:T(2,128)(2,1)}), bf16[8,2,24576]{2,1,0:T(2,128)(2,1)S(1)}, u32[]{:S(2)}, u32[]{:S(2)}) async-start(bf16[8,2,24576]{2,1,0:T(2,128)(2,1)} %reshape.47), calls=%async_computation.6 | async-start | bytes 1572864 | tf_op jit(solution)/shard_map/all_to_all | solution.py:100
  395.4 4.1 reshape.44
  405.8 5.3 %all-to-all-done.6 = bf16[8,2,24576]{2,1,0:T(2,128)(2,1)S(1)} async-done(((bf16[8,2,24576]{2,1,0:T(2,128)(2,1)}), bf16[8,2,24576]{2,1,0:T(2,128)(2,1)S(1)}, u32[]{:S(2)}, u32[]{:S(2)}) %all-to-all-start.6) | async-done | bytes 786464 | tf_op jit(solution)/shard_map/all_to_all | solution.py:100
  413.6 65.3 %reduce-scatter.4.cloned.1.call-done = bf16[192,384]{1,0:T(8,128)(2,1)} async-done(((bf16[6144,384]{1,0:T(8,128)(2,1)}), bf16[192,384]{1,0:T(8,128)(2,1)}) %reduce-scatter.4.cloned.1.call-update) | async-done | bytes 147472
  (114 shorter events, 64.6 us)
Async XLA Ops:
  29.4 27.5 %all-to-all-start = ((bf16[8,2,24576]{2,1,0:T(2,128)(2,1)}), bf16[8,2,24576]{2,1,0:T(2,128)(2,1)S(1)}, u32[]{:S(2)}, u32[]{:S(2)}) async-start(bf16[8,2,24576]{2,1,0:T(2,128)(2,1)} %reshape.37), calls=%async_computation | async-start | bytes 1572864 | tf_op jit(solution)/shard_map/all_to_all | solution.py:21
  57.0 26.8 %all-to-all-start.1 = ((bf16[8,2,24576]{2,1,0:T(2,128)(2,1)}), bf16[8,2,24576]{2,1,0:T(2,128)(2,1)}, u32[]{:S(2)}, u32[]{:S(2)}) async-start(bf16[8,2,24576]{2,1,0:T(2,128)(2,1)} %reshape.39), calls=%async_computation.1 | async-start | bytes 1572864 | tf_op jit(solution)/shard_map/all_to_all | solution.py:22
  106.7 156.5 %all-to-all-start.2 = ((bf16[8,1,128,6144]{3,2,1,0:T(8,128)(2,1)}), bf16[8,1,128,6144]{3,2,1,0:T(8,128)(2,1)}, u32[]{:S(2)}, u32[]{:S(2)}) async-start(bf16[8,1,128,6144]{3,2,1,0:T(8,128)(2,1)} %stack.2), calls=%async_computation.2 | async-start | bytes 25165824 | tf_op jit(solution)/shard_map/all_to_all | solution.py:12
  113.7 107.8 %all-gather.2.cloned.1.call-start = ((), (), s32[]{:S(2)}) async-start(), calls=%async_computation.8 | async-start | bytes 4866048 | tf_op jit(solution)/shard_map/all_gather | solution.py:17
  114.4 364.4 %reduce-scatter.4.cloned.1.call-start = ((), (), s32[]{:S(2)}) async-start(), calls=%async_computation.9 | async-start | bytes 4866048
  281.5 4.9 slice-start
  281.5 3.7 copy-start.5
  281.5 3.7 copy-start.10
  281.5 5.1 %slice-start.1 = ((s8[6291456]{0:T(1024)(128)(4,1)}), s8[2097152]{0:T(1024)(128)(4,1)S(1)}, s32[]{:S(2)}) async-start(s8[6291456]{0:T(1024)(128)(4,1)} %bitcast.145), calls=%async_computation.11 | async-start | bytes 4194304 | tf_op jit(solution)/shard_map/while
  289.0 4.0 copy-start
  289.0 4.0 copy-start.7
  293.0 2.4 copy-start.2
  293.0 2.4 copy-start.6
  295.4 1.0 copy-start.8
  296.4 1.2 copy-start.3
  304.2 4.9 slice-start
  304.2 3.7 copy-start.5
  304.2 3.7 copy-start.10
  304.2 5.1 %slice-start.1 = ((s8[6291456]{0:T(1024)(128)(4,1)}), s8[2097152]{0:T(1024)(128)(4,1)S(1)}, s32[]{:S(2)}) async-start(s8[6291456]{0:T(1024)(128)(4,1)} %bitcast.145), calls=%async_computation.11 | async-start | bytes 4194304 | tf_op jit(solution)/shard_map/while
  311.7 4.4 copy-start
  311.7 4.4 copy-start.7
  316.1 2.4 copy-start.2
  316.1 2.4 copy-start.6
  318.5 1.0 copy-start.8
  319.5 1.2 copy-start.3
  341.9 1.1 copy-start.9
  344.7 15.7 %copy-start.1 = (f32[1024,3,128]{0,2,1:T(8,128)S(1)}, f32[1024,3,128]{0,2,1:T(8,128)}, u32[]{:S(2)}) copy-start(f32[1024,3,128]{0,2,1:T(8,128)} %get-tuple-element.55) | copy-start | bytes 4718596
  354.0 20.9 %all-to-all-start.4 = ((bf16[8,2,24576]{2,1,0:T(2,128)(2,1)}), bf16[8,2,24576]{2,1,0:T(2,128)(2,1)}, u32[]{:S(2)}, u32[]{:S(2)}) async-start(bf16[8,2,24576]{2,1,0:T(2,128)(2,1)} %reshape.43), calls=%async_computation.4 | async-start | bytes 1572864 | tf_op jit(solution)/shard_map/all_to_all | solution.py:98
  365.7 15.2 %copy-start.4 = (f32[1024,3,128]{0,2,1:T(8,128)S(1)}, f32[1024,3,128]{0,2,1:T(8,128)}, u32[]{:S(2)}) copy-start(f32[1024,3,128]{0,2,1:T(8,128)} %get-tuple-element.56) | copy-start | bytes 4718596
  375.0 14.8 %all-to-all-start.5 = ((bf16[8,2,24576]{2,1,0:T(2,128)(2,1)}), bf16[8,2,24576]{2,1,0:T(2,128)(2,1)S(1)}, u32[]{:S(2)}, u32[]{:S(2)}) async-start(bf16[8,2,24576]{2,1,0:T(2,128)(2,1)} %reshape.45), calls=%async_computation.5 | async-start | bytes 1572864 | tf_op jit(solution)/shard_map/all_to_all | solution.py:99
  389.7 21.3 %all-to-all-start.6 = ((bf16[8,2,24576]{2,1,0:T(2,128)(2,1)}), bf16[8,2,24576]{2,1,0:T(2,128)(2,1)S(1)}, u32[]{:S(2)}, u32[]{:S(2)}) async-start(bf16[8,2,24576]{2,1,0:T(2,128)(2,1)} %reshape.47), calls=%async_computation.6 | async-start | bytes 1572864 | tf_op jit(solution)/shard_map/all_to_all | solution.py:100
Sparse Core Ops, SparseCore 0:
  117.3 104.2 all-gather.1
  342.0 136.8 reduce-scatter.3
